TPU v7x, 256 devices: a whole 4x4x8 slice. The times are simulated.
256 devices in a mesh: rep: 8 (over x, z_lo), mp: 32 (over z_hi, y, core).
Axes of the slice: x: 4, y: 4, z: 8 (z_hi: 4, z_lo: 2; z = z_hi * 2 + z_lo), core: 2. Of those that a mesh axis runs over, the one named last changes fastest.
Arguments:
- tokens: bfloat16 [8, 2048, 5120], P('rep', 'mp'), may hold values from -6 to 6
- prompt_ids: int32 [8, 2048], P('rep', 'mp'), may hold values from 0 to 11, never falling along the last dimension, each value on 1 to 512 neighbouring positions
- modulation: float32 [8, 12, 3, 5120], P('rep'), may hold values from -4 to 4
- trainer_up: float32 [5120, 13824], P('mp', 'rep'), may hold values from -0.078125 to 0.078125
- trainer_down: float32 [13824, 5120], P('rep', 'mp'), may hold values from -0.0546875 to 0.0546875
Outputs:
- result: bfloat16 [8, 2048, 5120], P('rep', 'mp')
Inputs may be any that keep to these rules, and one draw needn't show every extreme that they name: `prompt_ids`: along each replica's 2048 tokens the prompt number never falls; each of the 12 prompts has at least one token, and one prompt has exactly a quarter of 2048.
All inputs are finite; a program needn't handle non-finite values.
Results may differ from a plain program's by a relative error of at most 0.023.
Values may be sent and summed in bfloat16 or wider, within the bound.
A program may use at most 192 MiB of HBM per device.

v0:
```python
import jax
import jax.numpy as jnp
from jax import lax
from jax.sharding import PartitionSpec as P


def local(tokens, prompt_ids, modulation, trainer_up, trainer_down):
    as_float = tokens[0].astype(jnp.float32)
    average = jnp.mean(as_float, axis=-1, keepdims=True)
    centred = as_float - average
    variance = jnp.mean(centred * centred, axis=-1, keepdims=True)
    normed = centred / jnp.sqrt(variance + 1e-06)
    prompts_here = modulation.shape[1]
    onehot = (prompt_ids[0][:, None] == jnp.arange(prompts_here, dtype=jnp.int32)[None, :]).astype(
        jnp.float32
    )
    chosen = jnp.einsum("tp,pkd->tkd", onehot, modulation[0], precision=lax.Precision.HIGHEST)
    shift = chosen[:, 0]
    scale = chosen[:, 1]
    gate = chosen[:, 2]
    xin = (normed * (1.0 + scale) + shift).astype(jnp.bfloat16)
    up_half = trainer_up.astype(jnp.bfloat16)
    down_half = trainer_down.astype(jnp.bfloat16)
    up_rows = lax.all_gather(up_half, "rep", axis=1, tiled=True)
    w_up = lax.all_to_all(up_rows, "mp", split_axis=1, concat_axis=0, tiled=True)
    down_columns = lax.all_gather(down_half, "rep", axis=0, tiled=True)
    w_down = lax.all_to_all(down_columns, "mp", split_axis=0, concat_axis=1, tiled=True)
    hidden = jax.nn.gelu(
        jnp.dot(
            lax.all_gather(xin, "mp", axis=0, tiled=True), w_up, preferred_element_type=jnp.float32
        ),
        approximate=True,
    ).astype(jnp.bfloat16)
    mlp = lax.psum_scatter(
        jnp.dot(hidden, w_down, preferred_element_type=jnp.float32).astype(jnp.bfloat16),
        "mp",
        scatter_dimension=0,
        tiled=True,
    ).astype(jnp.float32)
    result = as_float + gate * mlp
    return result.astype(jnp.bfloat16)[None]


def solution(mesh):
    in_specs = (
        P("rep", "mp", None),
        P("rep", "mp"),
        P("rep", None, None, None),
        P("mp", "rep"),
        P("rep", "mp"),
    )
    out_specs = P("rep", "mp", None)
    return jax.shard_map(local, mesh=mesh, in_specs=in_specs, out_specs=out_specs, check_vma=False)
```

profile of v0, /device:TPU:1, one launch (start us, length us, event | category | flops | bytes accessed | tf_op | source)
XLA Modules:
  0.0 793.0 jit_solution(6808156185871499909)
XLA Ops:
  6.5 0.0 copy-start.1
  6.5 0.0 copy-start.3
  6.5 0.0 copy-start.2
  6.5 0.0 all-gather.8.cloned.1.call-start
  6.5 2.2 convert_bitcast_fusion.2
  8.8 0.0 all-gather.8.cloned.1.call-update
  8.8 0.0 all-gather.10.cloned.1.call-start
  8.8 2.1 convert_bitcast_fusion.1
  11.0 0.0 all-gather.10.cloned.1.call-update
  11.0 0.0 all-gather.6.cloned.1.call-start
  11.0 0.0 copy-done.1
  11.1 0.2 convert_reduce_fusion
  11.3 0.3 fusion.17
  11.6 0.0 copy-done.3
  11.6 0.0 copy-done.2
  11.6 1.8 fusion.24
  13.4 0.0 copy-start
  13.4 1.9 copy-done
  15.3 1.2 fusion.23
  16.5 0.0 all-gather.6.cloned.1.call-update
  16.5 96.8 %all-gather.8.cloned.1.call-done = bf16[8,1728,160]{1,2,0:T(8,128)(2,1)} async-done(((bf16[1,1728,160]{1,2,0:T(8,128)(2,1)}), bf16[8,1728,160]{1,2,0:T(8,128)(2,1)}) %all-gather.8.cloned.1.call-update) | async-done | bytes 4423696 | tf_op jit(solution)/shard_map/all_gather | solution.py:24
  113.3 7.0 copy.13
  120.3 8.6 %reshape.23 = bf16[13824,160]{0,1:T(8,128)(2,1)} reshape(bf16[8,1728,160]{1,0,2:T(8,128)(2,1)} %copy.13) | data formatting | bytes 8847360
  128.9 13.7 %all_to_all.28 = bf16[160,32,432]{2,1,0:T(8,128)(2,1)} reshape(bf16[160,13824]{1,0:T(8,128)(2,1)} %bitcast.79) | data formatting | bytes 8847360 | tf_op jit(solution)/shard_map/all_to_all | solution.py:25
  142.6 7.8 copy.14
  150.4 9.7 %all-to-all-start = ((bf16[160,32,432]{2,0,1:T(8,128)(2,1)}), bf16[160,32,432]{2,0,1:T(8,128)(2,1)}, u32[]{:S(2)}, u32[]{:S(2)}) async-start(bf16[160,32,432]{2,0,1:T(8,128)(2,1)} %copy.14), calls=%async_computation | async-start | bytes 10485760 | tf_op jit(solution)/shard_map/all_to_all | solution.py:25
  160.1 158.4 %all-gather.10.cloned.1.call-done = bf16[8,1728,160]{1,2,0:T(8,128)(2,1)} async-done(((bf16[1,1728,160]{1,2,0:T(8,128)(2,1)}), bf16[8,1728,160]{1,2,0:T(8,128)(2,1)}) %all-gather.10.cloned.1.call-update) | async-done | bytes 4423696 | tf_op jit(solution)/shard_map/all_gather | solution.py:26
  318.6 6.9 copy.15
  325.4 10.6 %all_to_all.32 = bf16[32,432,160]{1,0,2:T(8,128)(2,1)} reshape(bf16[8,1728,160]{1,0,2:T(8,128)(2,1)} %copy.15) | data formatting | bytes 8847360 | tf_op jit(solution)/shard_map/all_to_all | solution.py:27
  336.0 7.9 %copy.16 = bf16[32,432,160]{1,2,0:T(8,128)(2,1)} copy(bf16[32,432,160]{1,0,2:T(8,128)(2,1)} %all_to_all.32) | data formatting | bytes 8847360 | tf_op jit(solution)/shard_map/all_to_all | solution.py:27
  344.0 0.0 all-to-all-done
  344.0 11.5 %all-to-all-start.1 = ((bf16[32,432,160]{1,2,0:T(8,128)(2,1)}), bf16[32,432,160]{1,2,0:T(8,128)(2,1)}, u32[]{:S(2)}, u32[]{:S(2)}) async-start(bf16[32,432,160]{1,2,0:T(8,128)(2,1)} %copy.16), calls=%async_computation.1 | async-start | bytes 10485760 | tf_op jit(solution)/shard_map/all_to_all | solution.py:27
  355.5 0.3 reduce-scatter.2.cloned.1.call-start
  355.8 208.1 %all-gather.6.cloned.1.call-done = bf16[2048,5120]{1,0:T(8,128)(2,1)} async-done(((bf16[64,5120]{1,0:T(8,128)(2,1)}), bf16[2048,5120]{1,0:T(8,128)(2,1)}) %all-gather.6.cloned.1.call-update) | async-done | bytes 20971536 | tf_op jit(solution)/shard_map/all_gather | solution.py:30
  563.9 15.8 %fusion.49 = bf16[2048,432]{0,1:T(8,128)(2,1)S(1)} fusion(bf16[2048,5120]{1,0:T(8,128)(2,1)} %all-gather.6.cloned.1.call-done, bf16[5120,432]{1,0:T(8,128)(2,1)} %bitcast.11), kind=kOutput, calls=%fused_computation.9.clone.clone.1 | convolution fusion | flops 9067659264 | bytes 27164672 | tf_op jit(solution)/shard_map/dot_general | solution.py:29
  579.7 0.0 all-to-all-done.1
  579.7 16.8 %convolution_convert_fusion = bf16[2048,5120]{1,0:T(8,128)(2,1)} fusion(bf16[432,5120]{0,1:T(8,128)(2,1)} %bitcast.14, bf16[2048,432]{0,1:T(8,128)(2,1)S(1)} %fusion.49), kind=kOutput, calls=%fused_computation | convolution fusion | flops 9070182400 | bytes 27164672 | tf_op jit(solution)/shard_map/dot_general | solution.py:35
  596.5 0.0 reduce-scatter.2.cloned.1.call-update
  596.5 187.5 %reduce-scatter.2.cloned.1.call-done = bf16[64,5120]{1,0:T(8,128)(2,1)} async-done(((bf16[2048,5120]{1,0:T(8,128)(2,1)}), bf16[64,5120]{1,0:T(8,128)(2,1)}) %reduce-scatter.2.cloned.1.call-update) | async-done | bytes 655376 | tf_op jit(solution)/shard_map/reduce_scatter | solution.py:34
  783.9 2.6 fusion.27
  (2 shorter events, 0.0 us)
Async XLA Ops:
  6.5 4.5 copy-start.1
  6.5 5.1 copy-start.3
  6.5 5.1 copy-start.2
  6.5 106.8 %all-gather.8.cloned.1.call-start = ((), (), s32[]{:S(2)}) async-start(), calls=%async_computation.5 | async-start | bytes 5160960 | tf_op jit(solution)/shard_map/all_gather | solution.py:24
  8.8 309.8 %all-gather.10.cloned.1.call-start = ((), (), s32[]{:S(2)}) async-start(), calls=%async_computation.6 | async-start | bytes 5160960 | tf_op jit(solution)/shard_map/all_gather | solution.py:26
  11.0 552.9 %all-gather.6.cloned.1.call-start = ((), (), s32[]{:S(2)}) async-start(), calls=%async_computation.3 | async-start | bytes 21626880 | tf_op jit(solution)/shard_map/all_gather | solution.py:30
  13.4 1.9 copy-start
  150.4 193.6 %all-to-all-start = ((bf16[160,32,432]{2,0,1:T(8,128)(2,1)}), bf16[160,32,432]{2,0,1:T(8,128)(2,1)}, u32[]{:S(2)}, u32[]{:S(2)}) async-start(bf16[160,32,432]{2,0,1:T(8,128)(2,1)} %copy.14), calls=%async_computation | async-start | bytes 10485760 | tf_op jit(solution)/shard_map/all_to_all | solution.py:25
  344.0 235.7 %all-to-all-start.1 = ((bf16[32,432,160]{1,2,0:T(8,128)(2,1)}), bf16[32,432,160]{1,2,0:T(8,128)(2,1)}, u32[]{:S(2)}, u32[]{:S(2)}) async-start(bf16[32,432,160]{1,2,0:T(8,128)(2,1)} %copy.16), calls=%async_computation.1 | async-start | bytes 10485760 | tf_op jit(solution)/shard_map/all_to_all | solution.py:27
  355.5 428.4 %reduce-scatter.2.cloned.1.call-start = ((), (), s32[]{:S(2)}) async-start(), calls=%async_computation.4 | async-start | bytes 21626880 | tf_op jit(solution)/shard_map/reduce_scatter | solution.py:34
Sparse Core Ops, SparseCore 0:
  9.2 104.0 all-gather.7
  115.1 203.4 all-gather.9
  321.1 242.7 all-gather.5
  596.6 187.2 reduce-scatter.1
where the time goes:
time: 794 us; the launch traced here: 793 us
  waiting for transfers between devices  651 us (82%)
  local copies, waits for them, and re-layouts  64.4 us (8%)
  matrix products  34.3 us (4%)
  starting transfers between devices  21.5 us (3%)
  between operations  13.2 us (2%)
  other arithmetic  8.68 us (1%)
    all_gather x1, waiting for transfers between devices, local(): lax.all_gather(xin, 'mp', axis=0, tiled=True)  208 us
    reduce_scatter x1, waiting for transfers between devices, local(): lax.psum_scatter(jnp.dot(hidden, w_down, preferred_element_type=jnp.float...  187 us
    all_gather x1, waiting for transfers between devices, local(): down_columns = lax.all_gather(down_half, 'rep', axis=0, tiled=True)  158 us
    all_gather x1, waiting for transfers between devices, local(): up_rows = lax.all_gather(up_half, 'rep', axis=1, tiled=True)  96.8 us
    all_to_all x2, local copies, waits for them, and re-layouts, local(): lax.all_to_all(up_rows, 'mp', split_axis=1, concat_axis=0, tiled=True)  21.5 us
    all_to_all x2, local copies, waits for them, and re-layouts, local(): lax.all_to_all(down_columns, 'mp', split_axis=0, concat_axis=1, tiled=True)  18.6 us
    dot_general x1, matrix products, local(): jnp.dot(hidden, w_down, preferred_element_type=jnp.float32)  16.8 us
  transfers between devices with their start and end apart: 6, of which 4 were waited for; matrix products, arithmetic and copies ran while one was open for 8% of the time, Pallas kernels for 0%

commit v1 on v0

--- a/solution.py
+++ b/solution.py
@@ -5,6 +5,18 @@
 
 
 def local(tokens, prompt_ids, modulation, trainer_up, trainer_down):
+
+    def _turn_ratios(mat):
+        return jnp.concatenate(
+            lax.all_to_all(
+                jnp.stack([mat for _ in range(lax.axis_size("mp"))], axis=0),
+                axis_name="mp",
+                split_axis=0,
+                concat_axis=0,
+            ),
+            axis=0,
+        )
+
     as_float = tokens[0].astype(jnp.float32)
     average = jnp.mean(as_float, axis=-1, keepdims=True)
     centred = as_float - average
@@ -26,10 +38,7 @@
     down_columns = lax.all_gather(down_half, "rep", axis=0, tiled=True)
     w_down = lax.all_to_all(down_columns, "mp", split_axis=0, concat_axis=1, tiled=True)
     hidden = jax.nn.gelu(
-        jnp.dot(
-            lax.all_gather(xin, "mp", axis=0, tiled=True), w_up, preferred_element_type=jnp.float32
-        ),
-        approximate=True,
+        jnp.dot(_turn_ratios(xin), w_up, preferred_element_type=jnp.float32), approximate=True
     ).astype(jnp.bfloat16)
     mlp = lax.psum_scatter(
         jnp.dot(hidden, w_down, preferred_element_type=jnp.float32).astype(jnp.bfloat16),

time: 794 us -> 1170 us (1.47)
  waiting for transfers between devices: 651 us -> 1020 us
    all_gather x1 -> x0, waiting for transfers between devices: 208 us -> none  [local(): lax.all_gather(xin, 'mp', axis=0, tiled=True)]
    all_gather x1, waiting for transfers between devices: 158 us -> 337 us  [local(): down_columns = lax.all_gather(down_half, 'rep', axis=0, tiled=True)]
    all_to_all x0 -> x1, waiting for transfers between devices: none -> 174 us  [_turn_ratios(): lax.all_to_all(jnp.stack([mat for _ in range(lax.axis_size('mp'))], axis=...]
    all_to_all x1, waiting for transfers between devices: 0.01 us -> 111 us  [local(): lax.all_to_all(up_rows, 'mp', split_axis=1, concat_axis=0, tiled=True)]
    all_to_all x1, waiting for transfers between devices: 0.01 us -> 100 us  [local(): lax.all_to_all(down_columns, 'mp', split_axis=0, concat_axis=1, tiled=True)]
  transfers between devices with their start and end apart: 6 -> 6, of which waited for: 4 -> 6; matrix products, arithmetic and copies ran while one was open for 8% -> 3% of each run, Pallas kernels for 0% -> 0%
where the time goes in v1:
time: 1170 us
  waiting for transfers between devices  1020 us (87%)
  local copies, waits for them, and re-layouts  71.3 us (6%)
  matrix products  34.2 us (3%)
  starting transfers between devices  30.1 us (3%)
  between operations  13.2 us (1%)
    all_gather x1, waiting for transfers between devices, local(): down_columns = lax.all_gather(down_half, 'rep', axis=0, tiled=True)  337 us
    reduce_scatter x1, waiting for transfers between devices, local(): lax.psum_scatter(jnp.dot(hidden, w_down, preferred_element_type=jnp.float...  191 us
    all_to_all x1, waiting for transfers between devices, _turn_ratios(): lax.all_to_all(jnp.stack([mat for _ in range(lax.axis_size('mp'))], axis=...  174 us
    all_to_all x1, waiting for transfers between devices, local(): lax.all_to_all(up_rows, 'mp', split_axis=1, concat_axis=0, tiled=True)  111 us
    all_gather x1, waiting for transfers between devices, local(): up_rows = lax.all_gather(up_half, 'rep', axis=1, tiled=True)  105 us
    all_to_all x1, waiting for transfers between devices, local(): lax.all_to_all(down_columns, 'mp', split_axis=0, concat_axis=1, tiled=True)  100 us
  transfers between devices with their start and end apart: 6, of which 6 were waited for; matrix products, arithmetic and copies ran while one was open for 3% of the time, Pallas kernels for 0%

profile of v1, /device:TPU:1, one launch (start us, length us, event | category | flops | bytes accessed | tf_op | source)
XLA Modules:
  0.0 1173.0 jit_solution(6402995862321753696)
XLA Ops:
  6.5 0.0 all-gather.5.cloned.1.call-start
  6.5 2.1 convert_bitcast_fusion.2
  8.7 0.0 all-gather.5.cloned.1.call-update
  8.7 104.6 %all-gather.5.cloned.1.call-done = bf16[8,1728,160]{1,2,0:T(8,128)(2,1)} async-done(((bf16[1,1728,160]{1,2,0:T(8,128)(2,1)}), bf16[8,1728,160]{1,2,0:T(8,128)(2,1)}) %all-gather.5.cloned.1.call-update) | async-done | bytes 4423696 | tf_op jit(solution)/shard_map/all_gather | solution.py:36
  113.3 6.9 copy.13
  120.2 8.6 reshape.53
  128.8 13.6 %all_to_all.32 = bf16[160,32,432]{2,1,0:T(8,128)(2,1)} reshape(bf16[160,13824]{1,0:T(8,128)(2,1)} %bitcast.78) | data formatting | bytes 8847360 | tf_op jit(solution)/shard_map/all_to_all | solution.py:37
  142.4 7.7 copy.14
  150.2 0.0 copy-start.1
  150.2 0.0 copy-start.2
  150.2 0.0 copy-start.4
  150.2 9.8 all-to-all-start.1
  160.0 0.0 copy-done.1
  160.0 0.2 convert_reduce_fusion
  160.2 0.3 fusion.16
  160.6 0.0 copy-done.2
  160.6 0.0 copy-done.4
  160.6 1.8 fusion.24
  162.4 0.0 copy-start
  162.4 1.9 copy-done
  164.3 0.4 fusion.28
  164.7 110.5 %all-to-all-done.1 = bf16[160,32,432]{2,0,1:T(8,128)(2,1)} async-done(((bf16[160,32,432]{2,0,1:T(8,128)(2,1)}), bf16[160,32,432]{2,0,1:T(8,128)(2,1)}, u32[]{:S(2)}, u32[]{:S(2)}) %all-to-all-start.1) | async-done | bytes 4423712 | tf_op jit(solution)/shard_map/all_to_all | solution.py:37
  275.2 7.4 stack.5
  282.6 0.0 copy-start.3
  282.6 9.5 all-to-all-start
  292.1 0.0 all-gather.7.cloned.1.call-start
  292.1 0.0 copy-done.3
  292.2 0.9 convert_bitcast_fusion.1
  293.0 0.0 all-gather.7.cloned.1.call-update
  293.0 337.5 %all-gather.7.cloned.1.call-done = bf16[8,1728,160]{1,2,0:T(8,128)(2,1)} async-done(((bf16[1,1728,160]{1,2,0:T(8,128)(2,1)}), bf16[8,1728,160]{1,2,0:T(8,128)(2,1)}) %all-gather.7.cloned.1.call-update) | async-done | bytes 4423696 | tf_op jit(solution)/shard_map/all_gather | solution.py:38
  630.5 6.9 copy.15
  637.4 10.6 all_to_all.36
  648.0 7.7 copy.16
  655.7 174.0 %all-to-all-done = bf16[32,64,5120]{2,1,0:T(8,128)(2,1)} async-done(((bf16[32,64,5120]{2,1,0:T(8,128)(2,1)}), bf16[32,64,5120]{2,1,0:T(8,128)(2,1)}, u32[]{:S(2)}, u32[]{:S(2)}) %all-to-all-start) | async-done | bytes 20971552 | tf_op jit(solution)/shard_map/all_to_all | solution.py:11
  829.7 10.4 all-to-all-start.2
  840.2 0.3 reduce-scatter.2.cloned.1.call-start
  840.4 15.7 %fusion.50 = bf16[2048,432]{0,1:T(8,128)(2,1)S(1)} fusion(bf16[2048,5120]{1,0:T(8,128)(2,1)} %bitcast.8, bf16[5120,432]{1,0:T(8,128)(2,1)} %bitcast.13), kind=kOutput, calls=%fused_computation.9.clone.clone.1 | convolution fusion | flops 9067659264 | bytes 27164672 | tf_op jit(solution)/shard_map/dot_general | solution.py:41
  856.1 100.1 %all-to-all-done.2 = bf16[32,432,160]{1,2,0:T(8,128)(2,1)} async-done(((bf16[32,432,160]{1,2,0:T(8,128)(2,1)}), bf16[32,432,160]{1,2,0:T(8,128)(2,1)}, u32[]{:S(2)}, u32[]{:S(2)}) %all-to-all-start.2) | async-done | bytes 4423712 | tf_op jit(solution)/shard_map/all_to_all | solution.py:39
  956.2 16.8 %convolution_convert_fusion = bf16[2048,5120]{1,0:T(8,128)(2,1)} fusion(bf16[432,5120]{0,1:T(8,128)(2,1)} %bitcast.16, bf16[2048,432]{0,1:T(8,128)(2,1)S(1)} %fusion.50), kind=kOutput, calls=%fused_computation | convolution fusion | flops 9070182400 | bytes 27164672 | tf_op jit(solution)/shard_map/dot_general | solution.py:44
  972.9 0.0 reduce-scatter.2.cloned.1.call-update
  973.0 190.9 %reduce-scatter.2.cloned.1.call-done = bf16[64,5120]{1,0:T(8,128)(2,1)} async-done(((bf16[2048,5120]{1,0:T(8,128)(2,1)}), bf16[64,5120]{1,0:T(8,128)(2,1)}) %reduce-scatter.2.cloned.1.call-update) | async-done | bytes 655376 | tf_op jit(solution)/shard_map/reduce_scatter | solution.py:43
  1163.9 2.6 fusion.27
  (2 shorter events, 0.0 us)
Async XLA Ops:
  6.5 106.8 %all-gather.5.cloned.1.call-start = ((), (), s32[]{:S(2)}) async-start(), calls=%async_computation.5 | async-start | bytes 5160960 | tf_op jit(solution)/shard_map/all_gather | solution.py:36
  150.2 9.9 copy-start.1
  150.2 10.4 copy-start.2
  150.2 10.4 copy-start.4
  150.2 125.0 %all-to-all-start.1 = ((bf16[160,32,432]{2,0,1:T(8,128)(2,1)}), bf16[160,32,432]{2,0,1:T(8,128)(2,1)}, u32[]{:S(2)}, u32[]{:S(2)}) async-start(bf16[160,32,432]{2,0,1:T(8,128)(2,1)} %copy.14), calls=%async_computation.1 | async-start | bytes 10485760 | tf_op jit(solution)/shard_map/all_to_all | solution.py:37
  162.4 1.9 copy-start
  282.6 9.6 copy-start.3
  282.6 547.1 %all-to-all-start = ((bf16[32,64,5120]{2,1,0:T(8,128)(2,1)}), bf16[32,64,5120]{2,1,0:T(8,128)(2,1)}, u32[]{:S(2)}, u32[]{:S(2)}) async-start(bf16[32,64,5120]{2,1,0:T(8,128)(2,1)} %stack.5), calls=%async_computation | async-start | bytes 41943040 | tf_op jit(solution)/shard_map/all_to_all | solution.py:11
  292.1 338.4 %all-gather.7.cloned.1.call-start = ((), (), s32[]{:S(2)}) async-start(), calls=%async_computation.6 | async-start | bytes 5160960 | tf_op jit(solution)/shard_map/all_gather | solution.py:38
  829.7 126.5 %all-to-all-start.2 = ((bf16[32,432,160]{1,2,0:T(8,128)(2,1)}), bf16[32,432,160]{1,2,0:T(8,128)(2,1)}, u32[]{:S(2)}, u32[]{:S(2)}) async-start(bf16[32,432,160]{1,2,0:T(8,128)(2,1)} %copy.16), calls=%async_computation.2 | async-start | bytes 10485760 | tf_op jit(solution)/shard_map/all_to_all | solution.py:39
  840.2 323.8 %reduce-scatter.2.cloned.1.call-start = ((), (), s32[]{:S(2)}) async-start(), calls=%async_computation.4 | async-start | bytes 21626880 | tf_op jit(solution)/shard_map/reduce_scatter | solution.py:43
Sparse Core Ops, SparseCore 0:
  9.1 104.0 all-gather.4
  294.7 335.7 all-gather.6
  973.1 190.7 reduce-scatter.1
